TPU v7x, 32 devices: a whole 2x2x4 slice. The times are simulated.
32 devices in a mesh: dp: 4 (over y, core), tensor: 8 (over z, x).
Axes of the slice: x: 2, y: 2, z: 4, core: 2. Of those that a mesh axis runs over, the one named last changes fastest.
Arguments:
- tokens: bfloat16 [8192, 2048], P(('dp', 'tensor')), may hold values from -6 to 6
- gain_one: float32 [2048], replicated, may hold values from 0.5 to 1.5
- w_query: bfloat16 [2048, 256], P(None, 'tensor'), may hold values from -0.125 to 0.125
- w_key: bfloat16 [2048, 256], P(None, 'tensor'), may hold values from -0.125 to 0.125
- w_value: bfloat16 [2048, 2048], P(None, 'tensor'), may hold values from -0.125 to 0.125
- w_out: bfloat16 [2048, 2048], P('tensor'), may hold values from -0.5 to 0.5
- gain_two: float32 [2048], replicated, may hold values from 0.5 to 1.5
- w_gate: bfloat16 [2048, 5632], P(None, 'tensor'), may hold values from -0.125 to 0.125
- w_up: bfloat16 [2048, 5632], P(None, 'tensor'), may hold values from -0.125 to 0.125
- w_down: bfloat16 [5632, 2048], P('tensor'), may hold values from -0.078125 to 0.078125
- doc_ids: int32 [4, 2048], P('dp'), may hold values from 0 to 7, never falling along the last dimension, each value on 1 to 1024 neighbouring positions
- cotangent: bfloat16 [8192, 2048], P(('dp', 'tensor')), may hold values from -6 to 6
Outputs:
- block_out: bfloat16 [8192, 2048], P(('dp', 'tensor'))
- grad_tokens: float32 [8192, 2048], P(('dp', 'tensor'))
- grad_gain_one: float32 [2048], replicated
- grad_query: float32 [2048, 256], P(None, 'tensor')
- grad_key: float32 [2048, 256], P(None, 'tensor')
- grad_value: float32 [2048, 2048], P(None, 'tensor')
- grad_out_proj: float32 [2048, 2048], P('tensor')
- grad_gain_two: float32 [2048], replicated
- grad_gate: float32 [2048, 5632], P(None, 'tensor')
- grad_up: float32 [2048, 5632], P(None, 'tensor')
- grad_down: float32 [5632, 2048], P('tensor')
Inputs may be any that keep to these rules, and one draw needn't show every extreme that they name: Each row of doc_ids never falls along the row; each of the 8 documents of a group has 1 to 1024 tokens, and one has exactly 1024.
All inputs are finite; a program needn't handle non-finite values.
Results may differ from a plain program's by a relative error of at most 0.02.
Values may be sent and summed in bfloat16 or wider, within the bound.
No kernel may reach another device: no remote copies, remote signals or barrier semaphores. Data moves between devices by JAX's collectives and lax.ppermute only.
A program may use at most 256 MiB of HBM per device.

v0:
```python
import jax
import jax.numpy as jnp
from jax import lax
from jax.sharding import PartitionSpec as P

FEAT = 16
HEAD_V = 128
EPS = 1e-05


def norm_rows(values, gain_vec):
    row_scale = lax.rsqrt(jnp.mean(values * values, axis=-1, keepdims=True) + EPS)
    normed = values * row_scale
    return (normed, row_scale, (normed * gain_vec).astype(jnp.bfloat16))


def norm_back(grad_normed, normed, row_scale, gain_vec):
    weighted = grad_normed * gain_vec
    inner_mean = jnp.mean(weighted * normed, axis=-1, keepdims=True)
    return (row_scale * (weighted - normed * inner_mean), jnp.sum(grad_normed * normed, axis=0))


def contract_rows(left_mat, right_mat):
    return lax.dot_general(
        left_mat, right_mat, (((0,), (0,)), ((), ())), preferred_element_type=jnp.float32
    )


def times_transposed(left_mat, right_mat):
    return lax.dot_general(
        left_mat, right_mat, (((1,), (1,)), ((), ())), preferred_element_type=jnp.float32
    )


def block_kernel(query_rows, key_row_block, doc_row, row_start, block_rows):
    row_end_index = row_start + block_rows
    query_portion = query_rows[row_start:row_end_index]
    score_matrix = (
        jnp.einsum(
            "gsn,jsn->sgj",
            query_portion,
            key_row_block[:row_end_index],
            preferred_element_type=jnp.float32,
        )
        * 0.25
    )
    query_index = row_start + jnp.arange(block_rows)
    key_index = jnp.arange(row_end_index)
    allowed = (doc_row[row_start:row_end_index, None] == doc_row[None, :row_end_index]) & (
        query_index[:, None] >= key_index[None, :]
    )
    kernel = jnp.where(allowed[None], 1.0 + score_matrix + 0.5 * score_matrix * score_matrix, 0.0)
    return (score_matrix, allowed, kernel)


def attention_forward(query_rows, key_row_block, value_rows, doc_row, block_rows):
    group_rows = query_rows.shape[0]
    outputs = []
    denoms = []
    for row_start in range(0, group_rows, block_rows):
        row_end_index = row_start + block_rows
        score_matrix, allowed, kernel = block_kernel(
            query_rows, key_row_block, doc_row, row_start, block_rows
        )
        denominator = jnp.sum(kernel, axis=-1)
        numerator = jnp.einsum(
            "hqk,khd->qhd",
            kernel.astype(jnp.bfloat16),
            value_rows[:row_end_index],
            preferred_element_type=jnp.float32,
        )
        outputs.append((numerator / denominator.T[:, :, None]).astype(jnp.bfloat16))
        denoms.append(denominator)
    return (jnp.concatenate(outputs, axis=0), jnp.concatenate(denoms, axis=1))


def attention_backward(
    query_rows, key_row_block, value_rows, doc_row, denoms, grad_mixed, block_rows
):
    group_rows = query_rows.shape[0]
    grad_queries = []
    grad_keys = jnp.zeros(key_row_block.shape, jnp.float32)
    grad_values = jnp.zeros(value_rows.shape, jnp.float32)
    for row_start in range(0, group_rows, block_rows):
        row_end_index = row_start + block_rows
        score_matrix, allowed, kernel = block_kernel(
            query_rows, key_row_block, doc_row, row_start, block_rows
        )
        kernel_low = kernel.astype(jnp.bfloat16)
        denominator = denoms[:, row_start:row_end_index]
        numerator = jnp.einsum(
            "hqk,khd->qhd",
            kernel_low,
            value_rows[:row_end_index],
            preferred_element_type=jnp.float32,
        )
        grad_output = grad_mixed[row_start:row_end_index].astype(jnp.float32)
        grad_numer = (grad_output / denominator.T[:, :, None]).astype(jnp.bfloat16)
        grad_denom = -jnp.sum(grad_output * numerator, axis=-1).T / (denominator * denominator)
        grad_kernel = (
            jnp.einsum(
                "qhd,khd->hqk",
                grad_numer,
                value_rows[:row_end_index],
                preferred_element_type=jnp.float32,
            )
            + grad_denom[:, :, None]
        )
        score_gradients = jnp.where(allowed[None], grad_kernel * (1.0 + score_matrix), 0.0).astype(
            jnp.bfloat16
        )
        grad_queries.append(
            jnp.einsum(
                "zxu,uzc->xzc",
                score_gradients,
                key_row_block[:row_end_index],
                preferred_element_type=jnp.float32,
            )
            * 0.25
        )
        grad_keys = grad_keys.at[:row_end_index].add(
            jnp.einsum(
                "ari,ran->ian",
                score_gradients,
                query_rows[row_start:row_end_index],
                preferred_element_type=jnp.float32,
            )
            * 0.25
        )
        grad_values = grad_values.at[:row_end_index].add(
            jnp.einsum("hqk,qhd->khd", kernel_low, grad_numer, preferred_element_type=jnp.float32)
        )
    grad_query_rows = jnp.concatenate(grad_queries, axis=0).astype(jnp.bfloat16)
    return (grad_query_rows, grad_keys.astype(jnp.bfloat16), grad_values.astype(jnp.bfloat16))


def body(
    tokens,
    gain_one,
    w_query,
    w_key,
    w_value,
    w_out,
    gain_two,
    w_gate,
    w_up,
    w_down,
    doc_ids,
    cotangent,
):
    heads_here = w_query.shape[1] // FEAT
    doc_row = doc_ids[0]
    inputs = tokens.astype(jnp.float32)
    normed_one, scale_one, low_one = norm_rows(inputs, gain_one)
    gathered_one = lax.all_gather(low_one, "tensor", axis=0, tiled=True)
    group_rows = gathered_one.shape[0]
    block_rows = min(512, group_rows)
    query_flat = jnp.dot(gathered_one, w_query, preferred_element_type=jnp.float32).astype(
        jnp.bfloat16
    )
    key_flat = jnp.dot(gathered_one, w_key, preferred_element_type=jnp.float32).astype(jnp.bfloat16)
    value_flat = jnp.dot(gathered_one, w_value, preferred_element_type=jnp.float32).astype(
        jnp.bfloat16
    )
    query_rows = query_flat.reshape(group_rows, heads_here, FEAT)
    key_row_block = key_flat.reshape(group_rows, heads_here, FEAT)
    value_rows = value_flat.reshape(group_rows, heads_here, HEAD_V)
    mixed_blocks, denoms = attention_forward(
        query_rows, key_row_block, value_rows, doc_row, block_rows
    )
    mixed_heads = mixed_blocks.reshape(group_rows, heads_here * HEAD_V)
    part_rows = mixed_heads
    attn_out = lax.psum_scatter(
        jnp.dot(part_rows, w_out, preferred_element_type=jnp.float32),
        "tensor",
        scatter_dimension=0,
        tiled=True,
    )
    residual = inputs + attn_out
    normed_two, scale_two, low_two = norm_rows(residual, gain_two)
    gathered_two = lax.all_gather(low_two, "tensor", axis=0, tiled=True)
    gate_pre = jnp.dot(gathered_two, w_gate, preferred_element_type=jnp.float32)
    upward = jnp.dot(gathered_two, w_up, preferred_element_type=jnp.float32)
    sigmoid_gate = jax.nn.sigmoid(gate_pre)
    hidden = (gate_pre * sigmoid_gate * upward).astype(jnp.bfloat16)
    part_rows = hidden
    ffn_out = lax.psum_scatter(
        jnp.dot(part_rows, w_down, preferred_element_type=jnp.float32).astype(jnp.bfloat16),
        "tensor",
        scatter_dimension=0,
        tiled=True,
    ).astype(jnp.float32)
    block_out = (residual + ffn_out).astype(jnp.bfloat16)
    grad_rows = lax.all_gather(cotangent, "tensor", axis=0, tiled=True)
    grad_down_w = contract_rows(hidden, grad_rows)
    grad_hidden = times_transposed(grad_rows, w_down)
    slope_gate = sigmoid_gate * (1.0 + gate_pre * (1.0 - sigmoid_gate))
    grad_gate_act = (grad_hidden * upward * slope_gate).astype(jnp.bfloat16)
    grad_upward = (grad_hidden * (gate_pre * sigmoid_gate)).astype(jnp.bfloat16)
    grad_gate_w = contract_rows(gathered_two, grad_gate_act)
    grad_up_w = contract_rows(gathered_two, grad_upward)
    grad_normed_two = lax.psum_scatter(
        (times_transposed(grad_gate_act, w_gate) + times_transposed(grad_upward, w_up)).astype(
            jnp.bfloat16
        ),
        "tensor",
        scatter_dimension=0,
        tiled=True,
    ).astype(jnp.float32)
    grad_resid_norm, gain_two_part = norm_back(grad_normed_two, normed_two, scale_two, gain_two)
    grad_resid = cotangent.astype(jnp.float32) + grad_resid_norm
    grad_attn = grad_resid.astype(jnp.bfloat16)
    grad_attn_rows = lax.all_gather(grad_attn, "tensor", axis=0, tiled=True)
    grad_mixed = times_transposed(grad_attn_rows, w_out).astype(jnp.bfloat16)
    grad_out_w = contract_rows(mixed_heads, grad_attn_rows)
    grad_query_rows, grad_key_rows, grad_value_rows = attention_backward(
        query_rows,
        key_row_block,
        value_rows,
        doc_row,
        denoms,
        grad_mixed.reshape(group_rows, heads_here, HEAD_V),
        block_rows,
    )
    grad_query_flat = grad_query_rows.reshape(group_rows, heads_here * FEAT)
    grad_key_flat = grad_key_rows.reshape(group_rows, heads_here * FEAT)
    grad_value_flat = grad_value_rows.reshape(group_rows, heads_here * HEAD_V)
    grad_query_w = contract_rows(gathered_one, grad_query_flat)
    grad_key_w = contract_rows(gathered_one, grad_key_flat)
    grad_value_w = contract_rows(gathered_one, grad_value_flat)
    grad_normed_one = lax.psum_scatter(
        (
            times_transposed(grad_query_flat, w_query)
            + times_transposed(grad_key_flat, w_key)
            + times_transposed(grad_value_flat, w_value)
        ).astype(jnp.bfloat16),
        "tensor",
        scatter_dimension=0,
        tiled=True,
    ).astype(jnp.float32)
    grad_input_norm, gain_one_part = norm_back(grad_normed_one, normed_one, scale_one, gain_one)
    grad_tokens = grad_resid + grad_input_norm
    gain_grads = lax.psum((gain_one_part, gain_two_part), ("dp", "tensor"))
    weight_grads = (
        lax.psum(grad_query_w.astype(jnp.bfloat16), "dp").astype(jnp.float32),
        lax.psum(grad_key_w.astype(jnp.bfloat16), "dp").astype(jnp.float32),
        lax.psum(grad_value_w.astype(jnp.bfloat16), "dp").astype(jnp.float32),
        lax.psum(grad_out_w.astype(jnp.bfloat16), "dp").astype(jnp.float32),
        lax.psum(grad_gate_w.astype(jnp.bfloat16), "dp").astype(jnp.float32),
        lax.psum(grad_up_w.astype(jnp.bfloat16), "dp").astype(jnp.float32),
        lax.psum(grad_down_w.astype(jnp.bfloat16), "dp").astype(jnp.float32),
    )
    return (
        block_out,
        grad_tokens,
        gain_grads[0],
        weight_grads[0],
        weight_grads[1],
        weight_grads[2],
        weight_grads[3],
        gain_grads[1],
        weight_grads[4],
        weight_grads[5],
        weight_grads[6],
    )


def solution(mesh):
    in_specs = (
        P(("dp", "tensor"), None),
        P(),
        P(None, "tensor"),
        P(None, "tensor"),
        P(None, "tensor"),
        P("tensor", None),
        P(),
        P(None, "tensor"),
        P(None, "tensor"),
        P("tensor", None),
        P("dp", None),
        P(("dp", "tensor"), None),
    )
    out_specs = (
        P(("dp", "tensor"), None),
        P(("dp", "tensor"), None),
        P(),
        P(None, "tensor"),
        P(None, "tensor"),
        P(None, "tensor"),
        P("tensor", None),
        P(),
        P(None, "tensor"),
        P(None, "tensor"),
        P("tensor", None),
    )
    return jax.shard_map(body, mesh=mesh, in_specs=in_specs, out_specs=out_specs, check_vma=False)
```

profile of v0, /device:TPU:0, one launch (start us, length us, event | category | flops | bytes accessed | tf_op | source)
XLA Modules:
  0.0 1586.6 jit_solution(5318080155431390041)
XLA Ops:
  17.0 122.2 %all-gather.5.cloned.1.call-done = bf16[2048,2048]{1,0:T(8,128)(2,1)} async-done(((bf16[256,2048]{1,0:T(8,128)(2,1)}), bf16[2048,2048]{1,0:T(8,128)(2,1)}) %all-gather.5.cloned.1.call-update) | async-done | bytes 8388624 | tf_op jit(solution)/shard_map/all_gather | solution.py:155
  170.0 8.2 fusion.81
  178.7 280.7 %reduce-scatter.5.cloned.1.call-done = f32[256,2048]{1,0:T(8,128)} async-done(((f32[2048,2048]{1,0:T(8,128)}), f32[256,2048]{1,0:T(8,128)}) %reduce-scatter.5.cloned.1.call-update) | async-done | bytes 2097168 | tf_op jit(solution)/shard_map/reduce_scatter | solution.py:173
  464.8 123.5 %all-gather.7.cloned.1.call-done = bf16[2048,2048]{1,0:T(8,128)(2,1)} async-done(((bf16[256,2048]{1,0:T(8,128)(2,1)}), bf16[2048,2048]{1,0:T(8,128)(2,1)}) %all-gather.7.cloned.1.call-update) | async-done | bytes 8388624 | tf_op jit(solution)/shard_map/all_gather | solution.py:181
  588.3 11.2 fusion.83
  599.5 8.0 fusion.82
  607.5 106.2 %all-gather.9.cloned.1.call-done = bf16[2048,2048]{1,0:T(8,128)(2,1)} async-done(((bf16[256,2048]{1,0:T(8,128)(2,1)}), bf16[2048,2048]{1,0:T(8,128)(2,1)}) %all-gather.9.cloned.1.call-update) | async-done | bytes 8388624 | tf_op jit(solution)/shard_map/all_gather | solution.py:194
  713.7 14.6 multiply_convert_fusion
  728.3 10.5 fusion.84
  738.8 12.6 add_convert_fusion.1
  751.4 147.3 %reduce-scatter.9.cloned.1.call-done = bf16[256,2048]{1,0:T(8,128)(2,1)} async-done(((bf16[2048,2048]{1,0:T(8,128)(2,1)}), bf16[256,2048]{1,0:T(8,128)(2,1)}) %reduce-scatter.9.cloned.1.call-update) | async-done | bytes 1048592 | tf_op jit(solution)/shard_map/reduce_scatter | solution.py:202
  906.1 10.9 convolution_convert_fusion.1
  917.0 10.9 convolution_convert_fusion.2
  928.0 7.8 convolution_convert_fusion.3
  935.8 94.3 %all-gather.11.cloned.1.call-done = bf16[2048,2048]{1,0:T(8,128)(2,1)} async-done(((bf16[256,2048]{1,0:T(8,128)(2,1)}), bf16[2048,2048]{1,0:T(8,128)(2,1)}) %all-gather.11.cloned.1.call-update) | async-done | bytes 8388624 | tf_op jit(solution)/shard_map/all_gather | solution.py:213
  1030.1 6.1 convolution_convert_fusion.6
  1072.8 8.6 fusion.58
  1081.4 8.1 fusion.85
  1089.5 15.9 add_convert_fusion
  1105.4 11.0 convolution_convert_fusion
  1116.5 151.1 %all-reduce.6.cloned.1.call-done = (bf16[2048,32]{0,1:T(8,128)(2,1)}, bf16[2048,32]{0,1:T(8,128)(2,1)}, bf16[2048,256]{1,0:T(8,128)(2,1)}, bf16[256,2048]{1,0:T(...) async-done(((bf16[2048,32]{0,1:T(8,128)(2,1)}, bf16[2048,32]{0,1:T(8,128)(2,1)}, bf16[2048,256]{1,0:T(8,128)(2,1)}, ...) | async-done | bytes 11010064 | tf_op jit(solution)/shard_map/psum | solution.py:245
  1285.3 135.2 %reduce-scatter.11.cloned.1.call-done = bf16[256,2048]{1,0:T(8,128)(2,1)} async-done(((bf16[2048,2048]{1,0:T(8,128)(2,1)}), bf16[256,2048]{1,0:T(8,128)(2,1)}) %reduce-scatter.11.cloned.1.call-update) | async-done | bytes 1048592 | tf_op jit(solution)/shard_map/reduce_scatter | solution.py:231
  1422.9 42.8 %all-reduce.2 = (f32[2048]{0:T(1024)}, f32[2048]{0:T(1024)}) all-reduce(f32[2048]{0:T(1024)S(1)} %get-tuple-element.125, f32[2048]{0:T(1024)S(1)} %copy-done.56), channel_id=1, replica_groups=mesh['dp'=4,'tensor'=8] {'dp','tensor'}, use_global_device_ids=true, to_apply=%region_17.18 | all-reduce | flops 4096 | bytes 32768 | tf_op jit(solution)/shard_map/psum | solution.py:243
  1465.7 107.9 %reduce-scatter.7.cloned.1.call-done = bf16[256,2048]{1,0:T(8,128)(2,1)} async-done(((bf16[2048,2048]{1,0:T(8,128)(2,1)}), bf16[256,2048]{1,0:T(8,128)(2,1)}) %reduce-scatter.7.cloned.1.call-update) | async-done | bytes 1048592 | tf_op jit(solution)/shard_map/reduce_scatter | solution.py:187
  (288 shorter events, 115.4 us)
Async XLA Ops:
  7.2 706.5 %copy-start = (bf16[704,2048]{1,0:T(8,128)(2,1)S(1)}, bf16[704,2048]{1,0:T(8,128)(2,1)}, u32[]{:S(2)}) copy-start(bf16[704,2048]{1,0:T(8,128)(2,1)} %param.41) | copy-start | bytes 8650756
  7.2 132.1 %copy-start.25 = (bf16[2048,32]{0,1:T(8,128)(2,1)S(1)}, bf16[2048,32]{0,1:T(8,128)(2,1)}, u32[]{:S(2)}) copy-start(bf16[2048,32]{0,1:T(8,128)(2,1)} %param.35) | copy-start | bytes 393220
  7.2 132.0 %all-gather.5.cloned.1.call-start = ((), (), s32[]{:S(2)}) async-start(), calls=%async_computation.4 | async-start | bytes 9437184 | tf_op jit(solution)/shard_map/all_gather | solution.py:155
  11.5 447.9 %reduce-scatter.5.cloned.1.call-start = ((), (), s32[]{:S(2)}) async-start(), calls=%async_computation.5 | async-start | bytes 18874368 | tf_op jit(solution)/shard_map/reduce_scatter | solution.py:173
  13.1 142.0 %copy-start.27 = (pred[512,1024]{1,0:T(8,128)(4,1)}, pred[512,1024]{1,0:T(8,128)(4,1)S(1)}, u32[]{:S(2)}) copy-start(pred[512,1024]{1,0:T(8,128)(4,1)S(1)} %fusion.36) | copy-start | bytes 1572868
  145.4 17.2 %copy-start.11 = (bf16[2048,32]{0,1:T(8,128)(2,1)}, bf16[2048,32]{0,1:T(8,128)(2,1)S(1)}, u32[]{:S(2)}) copy-start(bf16[2048,32]{0,1:T(8,128)(2,1)S(1)} %convolution_convert_fusion.10) | copy-start | bytes 393220
  147.9 17.8 %copy-start.9 = (bf16[2048,256]{0,1:T(8,128)(2,1)}, bf16[2048,256]{0,1:T(8,128)(2,1)S(1)}, u32[]{:S(2)}) copy-start(bf16[2048,256]{0,1:T(8,128)(2,1)S(1)} %convolution_convert_fusion.7) | copy-start | bytes 3145732
  178.3 284.7 %copy-start.44 = (f32[2048]{0:T(1024)S(1)}, f32[2048]{0:T(1024)}, u32[]{:S(2)}) copy-start(f32[2048]{0:T(1024)} %param.38) | copy-start | bytes 24580
  178.3 410.0 %all-gather.7.cloned.1.call-start = ((), (), s32[]{:S(2)}) async-start(), calls=%async_computation.6 | async-start | bytes 9437184 | tf_op jit(solution)/shard_map/all_gather | solution.py:181
  461.6 440.5 %copy-start.57 = (f32[256]{0:T(256)}, f32[256]{0:T(256)S(1)}, u32[]{:S(2)}) copy-start(f32[256]{0:T(256)S(1)} %add_rsqrt_fusion) | copy-start | bytes 3076
  464.2 249.5 %all-gather.9.cloned.1.call-start = ((), (), s32[]{:S(2)}) async-start(), calls=%async_computation.8 | async-start | bytes 9437184 | tf_op jit(solution)/shard_map/all_gather | solution.py:194
  464.7 434.0 %reduce-scatter.9.cloned.1.call-start = ((), (), s32[]{:S(2)}) async-start(), calls=%async_computation.9 | async-start | bytes 9437184 | tf_op jit(solution)/shard_map/reduce_scatter | solution.py:202
  751.4 278.7 %all-gather.11.cloned.1.call-start = ((), (), s32[]{:S(2)}) async-start(), calls=%async_computation.10 | async-start | bytes 9437184 | tf_op jit(solution)/shard_map/all_gather | solution.py:213
  906.0 361.7 %all-reduce.6.cloned.1.call-start = ((), (), s32[]{:S(2)}) async-start(), calls=%async_computation.12 | async-start | bytes 22020096 | tf_op jit(solution)/shard_map/psum | solution.py:245
  906.1 21.9 %slice-start.5 = ((s8[8388608]{0:T(1024)(128)(4,1)}), s8[4194304]{0:T(1024)(128)(4,1)S(1)}, s32[]{:S(2)}) async-start(s8[8388608]{0:T(1024)(128)(4,1)} %bitcast.245), calls=%async_computation.18 | async-start | bytes 8388608
  935.8 100.6 %copy-start.70 = (f32[2,512]{1,0:T(2,128)S(1)}, f32[2,512]{1,0:T(2,128)}, u32[]{:S(2)}) copy-start(f32[2,512]{1,0:T(2,128)} %copy-done.69) | copy-start | bytes 12292
  1071.9 348.6 %reduce-scatter.11.cloned.1.call-start = ((), (), s32[]{:S(2)}) async-start(), calls=%async_computation.11 | async-start | bytes 9437184 | tf_op jit(solution)/shard_map/reduce_scatter | solution.py:231
  1105.4 468.3 %reduce-scatter.7.cloned.1.call-start = ((), (), s32[]{:S(2)}) async-start(), calls=%async_computation.7 | async-start | bytes 9437184 | tf_op jit(solution)/shard_map/reduce_scatter | solution.py:187
  1281.9 138.6 %copy-start.55 = (f32[2048]{0:T(1024)S(1)}, f32[2048]{0:T(1024)}, u32[]{:S(2)}) copy-start(f32[2048]{0:T(1024)} %param.33) | copy-start | bytes 24580
  1281.9 138.6 %copy-start.60 = (f32[256]{0:T(256)S(1)}, f32[256]{0:T(256)}, u32[]{:S(2)}) copy-start(f32[256]{0:T(256)} %copy-done.59) | copy-start | bytes 3076
  1281.9 140.9 %copy-start.56 = (f32[2048]{0:T(1024)S(1)}, f32[2048]{0:T(1024)}, u32[]{:S(2)}) copy-start(f32[2048]{0:T(1024)} %get-tuple-element.123) | copy-start | bytes 24580
  1282.0 291.7 %copy-start.45 = (f32[2048]{0:T(1024)S(1)}, f32[2048]{0:T(1024)}, u32[]{:S(2)}) copy-start(f32[2048]{0:T(1024)} %param.38) | copy-start | bytes 24580
  1282.0 291.7 %copy-start.58 = (f32[256]{0:T(256)S(1)}, f32[256]{0:T(256)}, u32[]{:S(2)}) copy-start(f32[256]{0:T(256)} %copy-done.57) | copy-start | bytes 3076
  1282.0 291.7 %copy-start.62 = (f32[256]{0:T(256)S(1)}, f32[256]{0:T(256)}, u32[]{:S(2)}) copy-start(f32[256]{0:T(256)} %copy-done.61) | copy-start | bytes 3076
  (81 other events, 383.9 us)
Sparse Core Ops, SparseCore 0:
  11.6 127.6 all-gather.4
  178.4 280.9 reduce-scatter.4
  464.3 123.9 all-gather.6
  590.5 123.1 all-gather.8
  751.5 147.1 reduce-scatter.8
  906.1 123.9 all-gather.10
  1072.0 195.5 all-reduce.5
  1271.3 149.1 reduce-scatter.10
  1424.6 149.0 reduce-scatter.6
where the time goes:
time: 1600 us; the launch traced here: 1590 us
  waiting for transfers between devices  1270 us (79%)
  matrix products  205 us (13%)
  other arithmetic  46.1 us (3%)
  blocking collectives  42.8 us (3%)
    reduce_scatter x1, waiting for transfers between devices, body(): lax.psum_scatter(jnp.dot(part_rows, w_out, preferred_element_type=jnp.flo...  281 us
    psum x1, waiting for transfers between devices, body(): lax.psum(grad_query_w.astype(jnp.bfloat16), 'dp').astype(jnp.float32)  151 us
    reduce_scatter x1, waiting for transfers between devices, body(): lax.psum_scatter((times_transposed(grad_gate_act, w_gate) + times_transpo...  147 us
    reduce_scatter x1, waiting for transfers between devices, body(): lax.psum_scatter((times_transposed(grad_query_flat, w_query) + times_tran...  135 us
    all_gather x1, waiting for transfers between devices, body(): gathered_two = lax.all_gather(low_two, 'tensor', axis=0, tiled=True)  124 us
    all_gather x1, waiting for transfers between devices, body(): gathered_one = lax.all_gather(low_one, 'tensor', axis=0, tiled=True)  122 us
    reduce_scatter x1, waiting for transfers between devices, body(): lax.psum_scatter(jnp.dot(part_rows, w_down, preferred_element_type=jnp.fl...  108 us
    all_gather x1, waiting for transfers between devices, body(): grad_rows = lax.all_gather(cotangent, 'tensor', axis=0, tiled=True)  106 us
  transfers between devices with their start and end apart: 9, of which 9 were waited for; matrix products, arithmetic and copies ran while one was open for 7% of the time, Pallas kernels for 0%

commit v1 on v0

--- a/solution.py
+++ b/solution.py
@@ -6,6 +6,32 @@
 FEAT = 16
 HEAD_V = 128
 EPS = 1e-05
+
+
+def return_all_keys_by_axis(array_here, peer_axis):
+    lower, v_next, w2 = (lax.psum(1, peer_axis), lax.axis_index(peer_axis), array_here.shape[0])
+    row_list = [t * lower if idx == 0 else t for idx, t in enumerate(array_here.shape)]
+    now = lax.dynamic_update_slice_in_dim(
+        jnp.zeros(row_list, array_here.dtype), array_here, v_next * w2, axis=0
+    )
+    base_arr = all_values = array_here
+    dev_j = 1
+    while dev_j < lower // 2 + 1:
+        base_arr = lax.ppermute(
+            base_arr, axis_name=peer_axis, perm=[(idx, (idx + 1) % lower) for idx in range(lower)]
+        )
+        now = lax.dynamic_update_slice_in_dim(now, base_arr, (v_next - dev_j) % lower * w2, axis=0)
+        if 2 * dev_j < lower:
+            all_values = lax.ppermute(
+                all_values,
+                axis_name=peer_axis,
+                perm=[(idx, (idx - 1) % lower) for idx in range(lower)],
+            )
+            now = lax.dynamic_update_slice_in_dim(
+                now, all_values, (v_next + dev_j) % lower * w2, axis=0
+            )
+        dev_j += 1
+    return now
 
 
 def norm_rows(values, gain_vec):
@@ -152,7 +178,7 @@
     doc_row = doc_ids[0]
     inputs = tokens.astype(jnp.float32)
     normed_one, scale_one, low_one = norm_rows(inputs, gain_one)
-    gathered_one = lax.all_gather(low_one, "tensor", axis=0, tiled=True)
+    gathered_one = return_all_keys_by_axis(low_one, "tensor")
     group_rows = gathered_one.shape[0]
     block_rows = min(512, group_rows)
     query_flat = jnp.dot(gathered_one, w_query, preferred_element_type=jnp.float32).astype(

time: 1600 us -> 1650 us (1.031)
  starting transfers between devices: 0.99 us -> 20.5 us
    ppermute x0 -> x7, waiting for transfers between devices: none -> 135 us  [the longest x4 119 us: return_all_keys_by_axis(): lax.ppermute(base_arr, axis_name=peer_axis, perm=[(idx, (idx + 1) % lower...]
    all_gather x1 -> x0, waiting for transfers between devices: 122 us -> none  [body(): gathered_one = lax.all_gather(low_one, 'tensor', axis=0, tiled=True)]
    ppermute x0 -> x7, starting transfers between devices: none -> 19.6 us  [the longest x4 10.4 us: return_all_keys_by_axis(): lax.ppermute(base_arr, axis_name=peer_axis, perm=[(idx, (idx + 1) % lower...]
  transfers between devices with their start and end apart: 9 -> 15, of which waited for: 9 -> 12; matrix products, arithmetic and copies ran while one was open for 7% -> 8% of each run, Pallas kernels for 0% -> 0%
where the time goes in v1:
time: 1650 us
  waiting for transfers between devices  1280 us (78%)
  matrix products  221 us (13%)
  blocking collectives  42.8 us (3%)
  other arithmetic  42.6 us (3%)
  local copies, waits for them, and re-layouts  22.5 us (1%)
  starting transfers between devices  20.5 us (1%)
    reduce_scatter x1, waiting for transfers between devices, body(): lax.psum_scatter(jnp.dot(part_rows, w_out, preferred_element_type=jnp.flo...  280 us
    psum x1, waiting for transfers between devices, body(): lax.psum(grad_query_w.astype(jnp.bfloat16), 'dp').astype(jnp.float32)  151 us
    reduce_scatter x1, waiting for transfers between devices, body(): lax.psum_scatter((times_transposed(grad_gate_act, w_gate) + times_transpo...  147 us
    reduce_scatter x1, waiting for transfers between devices, body(): lax.psum_scatter((times_transposed(grad_query_flat, w_query) + times_tran...  135 us
    all_gather x1, waiting for transfers between devices, body(): gathered_two = lax.all_gather(low_two, 'tensor', axis=0, tiled=True)  123 us
    ppermute x4, waiting for transfers between devices, return_all_keys_by_axis(): lax.ppermute(base_arr, axis_name=peer_axis, perm=[(idx, (idx + 1) % lower...  119 us
    reduce_scatter x1, waiting for transfers between devices, body(): lax.psum_scatter(jnp.dot(part_rows, w_down, preferred_element_type=jnp.fl...  108 us
    all_gather x1, waiting for transfers between devices, body(): grad_rows = lax.all_gather(cotangent, 'tensor', axis=0, tiled=True)  106 us
  transfers between devices with their start and end apart: 15, of which 12 were waited for; matrix products, arithmetic and copies ran while one was open for 8% of the time, Pallas kernels for 0%

profile of v1, /device:TPU:0, one launch (start us, length us, event | category | flops | bytes accessed | tf_op | source)
XLA Modules:
  0.0 1646.0 jit_solution(14260654749032856516)
XLA Ops:
  20.9 42.2 %collective-permute-done = bf16[256,2048]{1,0:T(8,128)(2,1)} collective-permute-done((bf16[256,2048]{1,0:T(8,128)(2,1)}, bf16[256,2048]{1,0:T(8,128)(2,1)}, u32[]{:S(2)}, u32[]{:S(2)}) %collective-permute-start) | collective-permute-done | bytes 1048608 | tf_op jit(solution)/shard_map/ppermute | solution.py:20
  69.8 40.1 %collective-permute-done.2 = bf16[256,2048]{1,0:T(8,128)(2,1)} collective-permute-done((bf16[256,2048]{1,0:T(8,128)(2,1)}, bf16[256,2048]{1,0:T(8,128)(2,1)}, u32[]{:S(2)}, u32[]{:S(2)}) %collective-permute-start.2) | collective-permute-done | bytes 1048608 | tf_op jit(solution)/shard_map/ppermute | solution.py:20
  119.6 36.3 %collective-permute-done.4 = bf16[256,2048]{1,0:T(8,128)(2,1)S(1)} collective-permute-done((bf16[256,2048]{1,0:T(8,128)(2,1)}, bf16[256,2048]{1,0:T(8,128)(2,1)S(1)}, u32[]{:S(2)}, u32[]{:S(2)}) %collective-permute-start.4) | collective-permute-done | bytes 1048608 | tf_op jit(solution)/shard_map/ppermute | solution.py:20
  165.3 16.6 %collective-permute-done.5 = bf16[256,2048]{1,0:T(8,128)(2,1)S(1)} collective-permute-done((bf16[256,2048]{1,0:T(8,128)(2,1)S(1)}, bf16[256,2048]{1,0:T(8,128)(2,1)S(1)}, u32[]{:S(2)}, u32[]{:S(2)}) %collective-permute-start.5) | collective-permute-done | bytes 1048608 | tf_op jit(solution)/shard_map/ppermute | solution.py:25
  222.2 8.2 fusion.82
  230.5 280.2 %reduce-scatter.5.cloned.1.call-done = f32[256,2048]{1,0:T(8,128)} async-done(((f32[2048,2048]{1,0:T(8,128)}), f32[256,2048]{1,0:T(8,128)}) %reduce-scatter.5.cloned.1.call-update) | async-done | bytes 2097168 | tf_op jit(solution)/shard_map/reduce_scatter | solution.py:199
  516.7 123.0 %all-gather.4.cloned.1.call-done = bf16[2048,2048]{1,0:T(8,128)(2,1)} async-done(((bf16[256,2048]{1,0:T(8,128)(2,1)}), bf16[2048,2048]{1,0:T(8,128)(2,1)}) %all-gather.4.cloned.1.call-update) | async-done | bytes 8388624 | tf_op jit(solution)/shard_map/all_gather | solution.py:207
  639.6 11.2 fusion.84
  658.8 106.3 %all-gather.6.cloned.1.call-done = bf16[2048,2048]{1,0:T(8,128)(2,1)} async-done(((bf16[256,2048]{1,0:T(8,128)(2,1)}), bf16[2048,2048]{1,0:T(8,128)(2,1)}) %all-gather.6.cloned.1.call-update) | async-done | bytes 8388624 | tf_op jit(solution)/shard_map/all_gather | solution.py:220
  765.1 14.6 multiply_convert_fusion
  779.8 10.5 fusion.85
  790.3 12.5 add_convert_fusion.1
  802.9 147.3 %reduce-scatter.9.cloned.1.call-done = bf16[256,2048]{1,0:T(8,128)(2,1)} async-done(((bf16[2048,2048]{1,0:T(8,128)(2,1)}), bf16[256,2048]{1,0:T(8,128)(2,1)}) %reduce-scatter.9.cloned.1.call-update) | async-done | bytes 1048592 | tf_op jit(solution)/shard_map/reduce_scatter | solution.py:228
  957.4 10.9 convolution_convert_fusion.1
  968.4 10.9 convolution_convert_fusion.2
  987.1 94.3 %all-gather.8.cloned.1.call-done = bf16[2048,2048]{1,0:T(8,128)(2,1)} async-done(((bf16[256,2048]{1,0:T(8,128)(2,1)}), bf16[2048,2048]{1,0:T(8,128)(2,1)}) %all-gather.8.cloned.1.call-update) | async-done | bytes 8388624 | tf_op jit(solution)/shard_map/all_gather | solution.py:239
  1132.1 8.6 fusion.58
  1140.7 8.1 fusion.86
  1148.8 15.9 add_convert_fusion
  1164.8 11.0 convolution_convert_fusion
  1175.8 151.1 %all-reduce.6.cloned.1.call-done = (bf16[2048,32]{0,1:T(8,128)(2,1)}, bf16[2048,32]{0,1:T(8,128)(2,1)}, bf16[2048,256]{1,0:T(8,128)(2,1)}, bf16[256,2048]{1,0:T(...) async-done(((bf16[2048,32]{0,1:T(8,128)(2,1)}, bf16[2048,32]{0,1:T(8,128)(2,1)}, bf16[2048,256]{1,0:T(8,128)(2,1)}, ...) | async-done | bytes 11010064 | tf_op jit(solution)/shard_map/psum | solution.py:271
  1344.6 135.2 %reduce-scatter.11.cloned.1.call-done = bf16[256,2048]{1,0:T(8,128)(2,1)} async-done(((bf16[2048,2048]{1,0:T(8,128)(2,1)}), bf16[256,2048]{1,0:T(8,128)(2,1)}) %reduce-scatter.11.cloned.1.call-update) | async-done | bytes 1048592 | tf_op jit(solution)/shard_map/reduce_scatter | solution.py:257
  1482.2 42.8 %all-reduce.2 = (f32[2048]{0:T(1024)}, f32[2048]{0:T(1024)}) all-reduce(f32[2048]{0:T(1024)S(1)} %get-tuple-element.125, f32[2048]{0:T(1024)S(1)} %copy-done.57), channel_id=1, replica_groups=mesh['dp'=4,'tensor'=8] {'dp','tensor'}, use_global_device_ids=true, to_apply=%region_17.18 | all-reduce | flops 4096 | bytes 32768 | tf_op jit(solution)/shard_map/psum | solution.py:269
  1525.0 107.9 %reduce-scatter.7.cloned.1.call-done = bf16[256,2048]{1,0:T(8,128)(2,1)} async-done(((bf16[2048,2048]{1,0:T(8,128)(2,1)}), bf16[256,2048]{1,0:T(8,128)(2,1)}) %reduce-scatter.7.cloned.1.call-update) | async-done | bytes 1048592 | tf_op jit(solution)/shard_map/reduce_scatter | solution.py:213
  (304 shorter events, 184.5 us)
Async XLA Ops:
  7.2 758.0 %copy-start = (bf16[704,2048]{1,0:T(8,128)(2,1)S(1)}, bf16[704,2048]{1,0:T(8,128)(2,1)}, u32[]{:S(2)}) copy-start(bf16[704,2048]{1,0:T(8,128)(2,1)} %param.41) | copy-start | bytes 8650756
  7.2 503.5 %reduce-scatter.5.cloned.1.call-start = ((), (), s32[]{:S(2)}) async-start(), calls=%async_computation.4 | async-start | bytes 18874368 | tf_op jit(solution)/shard_map/reduce_scatter | solution.py:199
  15.0 48.2 %collective-permute-start = (bf16[256,2048]{1,0:T(8,128)(2,1)}, bf16[256,2048]{1,0:T(8,128)(2,1)}, u32[]{:S(2)}, u32[]{:S(2)}) collective-permute-start(bf16[256,2048]{1,0:T(8,128)(2,1)} %get-tuple-element.143), channel_id=1, source_target_pairs={{0,1},{1,2},{2,3},{3,4},{4,5},{5,6},{6,7},{7,0},{8,9},{9,10},{10,1... | collective-permute-start | bytes 3145736 | tf_op jit(solution)/shard_map/ppermute | solution.py:20
  17.9 48.6 %collective-permute-start.1 = (bf16[256,2048]{1,0:T(8,128)(2,1)}, bf16[256,2048]{1,0:T(8,128)(2,1)}, u32[]{:S(2)}, u32[]{:S(2)}) collective-permute-start(bf16[256,2048]{1,0:T(8,128)(2,1)} %get-tuple-element.143), channel_id=1, source_target_pairs={{0,7},{1,0},{2,1},{3,2},{4,3},{5,4},{6,5},{7,6},{8,15},{9,8},{10,9... | collective-permute-start | bytes 3145736 | tf_op jit(solution)/shard_map/ppermute | solution.py:25
  63.1 46.8 %collective-permute-start.2 = (bf16[256,2048]{1,0:T(8,128)(2,1)}, bf16[256,2048]{1,0:T(8,128)(2,1)}, u32[]{:S(2)}, u32[]{:S(2)}) collective-permute-start(bf16[256,2048]{1,0:T(8,128)(2,1)} %collective-permute-done), channel_id=1, source_target_pairs={{0,1},{1,2},{2,3},{3,4},{4,5},{5,6},{6,7},{7,0},{8,9},{9,10},{10,1... | collective-permute-start | bytes 3145736 | tf_op jit(solution)/shard_map/ppermute | solution.py:20
  66.5 145.5 %copy-start.19 = (pred[512,1536]{1,0:T(8,128)(4,1)}, pred[512,1536]{1,0:T(8,128)(4,1)S(1)}, u32[]{:S(2)}) copy-start(pred[512,1536]{1,0:T(8,128)(4,1)S(1)} %fusion.10) | copy-start | bytes 2359300
  66.5 47.7 %collective-permute-start.3 = (bf16[256,2048]{1,0:T(8,128)(2,1)}, bf16[256,2048]{1,0:T(8,128)(2,1)S(1)}, u32[]{:S(2)}, u32[]{:S(2)}) collective-permute-start(bf16[256,2048]{1,0:T(8,128)(2,1)} %collective-permute-done.1), channel_id=1, source_target_pairs={{0,7},{1,0},{2,1},{3,2},{4,3},{5,4},{6,5},{7,6},{8,15},{9,8},{10,9... | collective-permute-start | bytes 3145736 | tf_op jit(solution)/shard_map/ppermute | solution.py:25
  109.9 45.9 %collective-permute-start.4 = (bf16[256,2048]{1,0:T(8,128)(2,1)}, bf16[256,2048]{1,0:T(8,128)(2,1)S(1)}, u32[]{:S(2)}, u32[]{:S(2)}) collective-permute-start(bf16[256,2048]{1,0:T(8,128)(2,1)} %collective-permute-done.2), channel_id=1, source_target_pairs={{0,1},{1,2},{2,3},{3,4},{4,5},{5,6},{6,7},{7,0},{8,9},{9,10},{10,1... | collective-permute-start | bytes 3145736 | tf_op jit(solution)/shard_map/ppermute | solution.py:20
  114.2 67.7 %collective-permute-start.5 = (bf16[256,2048]{1,0:T(8,128)(2,1)S(1)}, bf16[256,2048]{1,0:T(8,128)(2,1)S(1)}, u32[]{:S(2)}, u32[]{:S(2)}) collective-permute-start(bf16[256,2048]{1,0:T(8,128)(2,1)S(1)} %collective-permute-done.3), channel_id=1, source_target_pairs={{0,7},{1,0},{2,1},{3,2},{4,3},{5,4},{6,5},{7,6},{8,15},{9,8},{10,9... | collective-permute-start | bytes 3145736 | tf_op jit(solution)/shard_map/ppermute | solution.py:25
  155.9 27.1 %collective-permute-start.6 = (bf16[256,2048]{1,0:T(8,128)(2,1)S(1)}, bf16[256,2048]{1,0:T(8,128)(2,1)S(1)}, u32[]{:S(2)}, u32[]{:S(2)}) collective-permute-start(bf16[256,2048]{1,0:T(8,128)(2,1)S(1)} %collective-permute-done.4), channel_id=1, source_target_pairs={{0,1},{1,2},{2,3},{3,4},{4,5},{5,6},{6,7},{7,0},{8,9},{9,10},{10,1... | collective-permute-start | bytes 3145736 | tf_op jit(solution)/shard_map/ppermute | solution.py:20
  230.5 283.8 %copy-start.44 = (f32[2048]{0:T(1024)S(1)}, f32[2048]{0:T(1024)}, u32[]{:S(2)}) copy-start(f32[2048]{0:T(1024)} %param.38) | copy-start | bytes 24580
  230.5 409.2 %all-gather.4.cloned.1.call-start = ((), (), s32[]{:S(2)}) async-start(), calls=%async_computation.5 | async-start | bytes 9437184 | tf_op jit(solution)/shard_map/all_gather | solution.py:207
  512.9 440.7 %copy-start.58 = (f32[256]{0:T(256)}, f32[256]{0:T(256)S(1)}, u32[]{:S(2)}) copy-start(f32[256]{0:T(256)S(1)} %add_rsqrt_fusion) | copy-start | bytes 3076
  515.5 249.7 %all-gather.6.cloned.1.call-start = ((), (), s32[]{:S(2)}) async-start(), calls=%async_computation.7 | async-start | bytes 9437184 | tf_op jit(solution)/shard_map/all_gather | solution.py:220
  516.2 434.0 %reduce-scatter.9.cloned.1.call-start = ((), (), s32[]{:S(2)}) async-start(), calls=%async_computation.8 | async-start | bytes 9437184 | tf_op jit(solution)/shard_map/reduce_scatter | solution.py:228
  802.9 278.6 %all-gather.8.cloned.1.call-start = ((), (), s32[]{:S(2)}) async-start(), calls=%async_computation.9 | async-start | bytes 9437184 | tf_op jit(solution)/shard_map/all_gather | solution.py:239
  957.4 369.6 %all-reduce.6.cloned.1.call-start = ((), (), s32[]{:S(2)}) async-start(), calls=%async_computation.11 | async-start | bytes 22020096 | tf_op jit(solution)/shard_map/psum | solution.py:271
  1131.3 348.6 %reduce-scatter.11.cloned.1.call-start = ((), (), s32[]{:S(2)}) async-start(), calls=%async_computation.10 | async-start | bytes 9437184 | tf_op jit(solution)/shard_map/reduce_scatter | solution.py:257
  1164.7 468.2 %reduce-scatter.7.cloned.1.call-start = ((), (), s32[]{:S(2)}) async-start(), calls=%async_computation.6 | async-start | bytes 9437184 | tf_op jit(solution)/shard_map/reduce_scatter | solution.py:213
  1341.3 138.6 %copy-start.61 = (f32[256]{0:T(256)S(1)}, f32[256]{0:T(256)}, u32[]{:S(2)}) copy-start(f32[256]{0:T(256)} %copy-done.60) | copy-start | bytes 3076
  1341.3 140.9 %copy-start.57 = (f32[2048]{0:T(1024)S(1)}, f32[2048]{0:T(1024)}, u32[]{:S(2)}) copy-start(f32[2048]{0:T(1024)} %get-tuple-element.123) | copy-start | bytes 24580
  1341.3 291.7 %copy-start.45 = (f32[2048]{0:T(1024)S(1)}, f32[2048]{0:T(1024)}, u32[]{:S(2)}) copy-start(f32[2048]{0:T(1024)} %param.38) | copy-start | bytes 24580
  1341.3 291.7 %copy-start.59 = (f32[256]{0:T(256)S(1)}, f32[256]{0:T(256)}, u32[]{:S(2)}) copy-start(f32[256]{0:T(256)} %copy-done.58) | copy-start | bytes 3076
  1341.3 291.7 %copy-start.63 = (f32[256]{0:T(256)S(1)}, f32[256]{0:T(256)}, u32[]{:S(2)}) copy-start(f32[256]{0:T(256)} %copy-done.62) | copy-start | bytes 3076
  (86 other events, 1227.9 us)
Sparse Core Ops, SparseCore 0:
  230.6 280.0 reduce-scatter.4
  515.6 124.0 all-gather.3
  642.0 123.1 all-gather.5
  803.0 147.1 reduce-scatter.8
  957.5 123.9 all-gather.7
  1131.4 195.5 all-reduce.5
  1330.6 149.1 reduce-scatter.10
  1483.9 149.0 reduce-scatter.6
